TPU v7x, 32 devices: a whole 2x2x4 slice. The times are simulated.
32 devices in a mesh: groups: 2 (over y), ctx: 16 (over z, x, core).
Axes of the slice: x: 2, y: 2, z: 4, core: 2. Of those that a mesh axis runs over, the one named last changes fastest.
Arguments:
- self_qkv: bfloat16 [3, 8192, 2048], P(None, ('groups', 'ctx')), parts along dimension 1, may hold values from -64 to 64
- windows: int32 [16], replicated, may hold values from 256 to 2048, as said below
- k_gain: float32 [2048], replicated, may hold values from 0.25 to 1.75
- cont_qkv: bfloat16 [3, 256, 2048], P(None, ('groups', 'ctx')), parts along dimension 1, may hold values from -64 to 64
- starts: int32 [32], P('groups'), parts along dimension 0, may hold values from 1 to 4096
Outputs:
- self_out: bfloat16 [8192, 2048], P(('groups', 'ctx')), parts along dimension 0
- cross_out: bfloat16 [256, 2048], P(('groups', 'ctx')), parts along dimension 0
There are 2 independent parts, one for each index of `groups`. A program takes and returns all parts, laid end to end along the dimension named above; an argument that names none is the same for every part. Nothing has to cross between parts.
Inputs may be any that keep to these rules, and one draw needn't show every extreme that they name: `windows`: some head has a window of exactly 2048.
All inputs are finite; a program needn't handle non-finite values.
Results may differ from a plain program's by a relative error of at most 0.0055.
Values may be sent and summed in bfloat16 or wider, within the bound.
No kernel may reach another device: no remote copies, remote signals or barrier semaphores. Data moves between devices by JAX's collectives and lax.ppermute only.
A program may use at most 128 MiB of HBM per device.

v0:
```python
import math
import jax
import jax.numpy as jnp
from jax import lax
from jax.sharding import PartitionSpec as P

WIN = 2048
CLEN = 8
EPSILON = 1e-06
NEGATIVE = -1e30


def shifted(value, axis, steps):
    count = lax.axis_size(axis)
    initial, last = (max(0, -steps), min(count, count - steps))
    return lax.ppermute(value, axis, [(source, source + steps) for source in range(initial, last)])


def finish_rows(cache_high, cache_totals, weighted, own_rows):
    rows_here = own_rows.shape[1]
    features = own_rows.shape[2]
    head_count = cache_high.shape[1]
    head_dim = features // head_count
    groups_here = rows_here // CLEN
    parts = own_rows.reshape(3, groups_here, CLEN, head_count, head_dim)
    scaling = 1.0 / math.sqrt(head_dim)
    scores = (
        jnp.einsum("cihd,cjhd->hcij", parts[0], parts[1], preferred_element_type=jnp.float32)
        * scaling
    )
    causal = (jnp.arange(CLEN)[None, :] <= jnp.arange(CLEN)[:, None])[None, None]
    scores = jnp.where(causal, scores, NEGATIVE)
    prior_high = cache_high.T.reshape(head_count, groups_here, CLEN)
    final = jnp.maximum(prior_high, jnp.max(scores, axis=-1))
    rescale = jnp.exp(prior_high - final)
    expo = jnp.where(causal, jnp.exp(scores - final[..., None]), 0.0)
    totals = rescale * cache_totals.T.reshape(head_count, groups_here, CLEN) + jnp.sum(
        expo, axis=-1
    )
    own_sum = jnp.einsum(
        "hcij,cjhd->cihd", expo.astype(jnp.bfloat16), parts[2], preferred_element_type=jnp.float32
    )
    merged = (
        weighted.reshape(groups_here, CLEN, head_count, head_dim)
        * jnp.transpose(rescale, (1, 2, 0))[..., None]
        + own_sum
    )
    result = merged / jnp.transpose(totals, (1, 2, 0))[..., None]
    return result.reshape(rows_here, features).astype(jnp.bfloat16)


def per_device(self_qkv, windows, k_gain, cont_qkv, starts):
    length = self_qkv.shape[1]
    features = self_qkv.shape[2]
    head_count = windows.shape[0]
    head_dim = features // head_count
    scaling = 1.0 / math.sqrt(head_dim)
    anchor = lax.axis_index("ctx") * length
    reach = WIN // length
    width = (reach + 1) * length
    key_value = self_qkv[1:3]
    earlier = []
    for distance in range(1, reach + 1):
        earlier.append(shifted(key_value, "ctx", distance))
    band = jnp.concatenate(earlier[::-1] + [key_value], axis=1)
    distance_grid = (
        jnp.arange(length, dtype=jnp.int32)[:, None]
        + reach * length
        - jnp.arange(width, dtype=jnp.int32)[None, :]
    )
    key_position = anchor - reach * length + jnp.arange(width, dtype=jnp.int32)

    def one_head(head):
        offset = head * head_dim
        queries = lax.dynamic_slice_in_dim(self_qkv[0], offset, head_dim, 1)
        keys = lax.dynamic_slice_in_dim(band[0], offset, head_dim, 1)
        values = lax.dynamic_slice_in_dim(band[1], offset, head_dim, 1)
        scores = (
            jnp.einsum("id,jd->ij", queries, keys, preferred_element_type=jnp.float32) * scaling
        )
        visible = (
            (distance_grid >= 0) & (distance_grid < windows[head]) & (key_position >= 0)[None, :]
        )
        scores = jnp.where(visible, scores, NEGATIVE)
        highest = jnp.max(scores, axis=-1, keepdims=True)
        expo = jnp.where(visible, jnp.exp(scores - highest), 0.0)
        weights = (expo / jnp.sum(expo, axis=-1, keepdims=True)).astype(jnp.bfloat16)
        return jnp.dot(weights, values, preferred_element_type=jnp.float32).astype(jnp.bfloat16)

    attended = lax.map(one_head, jnp.arange(head_count, dtype=jnp.int32))
    self_out = jnp.transpose(attended, (1, 0, 2)).reshape(length, features)
    hidden = self_out.astype(jnp.float32).reshape(length, head_count, head_dim)
    normed = hidden * lax.rsqrt(jnp.mean(hidden * hidden, axis=-1, keepdims=True) + EPSILON)
    cache_keys = (
        (normed.reshape(length, features) * k_gain)
        .astype(jnp.bfloat16)
        .reshape(length, head_count, head_dim)
    )
    cache_values = self_out.reshape(length, head_count, head_dim)
    gathered = lax.all_gather(cont_qkv[0], "ctx", axis=0, tiled=True)
    rows_all = gathered.shape[0]
    rows_here = cont_qkv.shape[1]
    conts_all = starts.shape[0]
    row_start = jnp.broadcast_to(starts[:, None], (conts_all, rows_all // conts_all)).reshape(
        rows_all
    )
    positions = anchor + jnp.arange(length, dtype=jnp.int32)
    block = math.gcd(rows_all, 512)
    block_count = rows_all // block
    query_blocks = gathered.reshape(block_count, block, head_count, head_dim)
    start_blocks = row_start.reshape(block_count, block)

    def block_scores(query_block, start_block):
        raw = (
            jnp.einsum("ihd,jhd->hij", query_block, cache_keys, preferred_element_type=jnp.float32)
            * scaling
        )
        seen = (positions[None, :] < start_block[:, None])[None]
        return (jnp.where(seen, raw, NEGATIVE), seen)

    def local_part(inputs):
        query_block, start_block = inputs
        masked, seen = block_scores(query_block, start_block)
        peak = jnp.max(masked, axis=-1)
        local_expo = jnp.where(seen, jnp.exp(masked - peak[..., None]), 0.0)
        totals = jnp.sum(local_expo, axis=-1)
        summed = jnp.einsum(
            "hij,jhd->ihd",
            local_expo.astype(jnp.bfloat16),
            cache_values,
            preferred_element_type=jnp.float32,
        )
        return (summed.reshape(block, features), peak.T, totals.T)

    summed, peaks, totals = lax.map(local_part, (query_blocks, start_blocks))
    sources = lax.axis_size("ctx")
    summed = summed.reshape(sources, rows_here, features)
    peaks = peaks.reshape(sources, rows_here, head_count)
    totals = totals.reshape(sources, rows_here, head_count)
    summed_in, peaks_in, totals_in = (
        lax.all_to_all(
            summed.astype(jnp.bfloat16), "ctx", split_axis=0, concat_axis=0, tiled=True
        ).astype(summed.dtype),
        lax.all_to_all(
            peaks.astype(jnp.bfloat16), "ctx", split_axis=0, concat_axis=0, tiled=True
        ).astype(peaks.dtype),
        lax.all_to_all(
            totals.astype(jnp.bfloat16), "ctx", split_axis=0, concat_axis=0, tiled=True
        ).astype(totals.dtype),
    )
    cache_high = jnp.max(peaks_in, axis=0)
    rescale = jnp.exp(peaks_in - cache_high[None])
    weighted = jnp.sum(
        summed_in.reshape(sources, rows_here, head_count, head_dim) * rescale[..., None], axis=0
    )
    cache_totals = jnp.sum(rescale * totals_in, axis=0)
    cross_out = finish_rows(cache_high, cache_totals, weighted, cont_qkv)
    return (self_out, cross_out)


def solution(mesh):
    in_specs = (
        P(None, ("groups", "ctx"), None),
        P(),
        P(),
        P(None, ("groups", "ctx"), None),
        P("groups"),
    )
    out_specs = (P(("groups", "ctx"), None), P(("groups", "ctx"), None))
    return jax.shard_map(
        per_device, mesh=mesh, in_specs=in_specs, out_specs=out_specs, check_vma=False
    )
```

profile of v0, /device:TPU:0, one launch (start us, length us, event | category | flops | bytes accessed | tf_op | source)
XLA Modules:
  0.0 854.6 jit_solution(9346026822741052805)
XLA Ops:
  3.9 7.3 collective-permute-start
  23.8 32.4 %collective-permute-done = bf16[2,256,2048]{2,1,0:T(8,128)(2,1)} collective-permute-done((bf16[2,256,2048]{2,1,0:T(8,128)(2,1)}, bf16[2,256,2048]{2,1,0:T(8,128)(2,1)}, u32[]{:S(2)}, u32[]{:S(2)}) %collective-permute-start) | collective-permute-done | bytes 2097184 | tf_op jit(solution)/shard_map/ppermute | solution.py:16
  59.1 301.0 %all-gather = bf16[1,128,2048]{2,1,0:T(8,128)(2,1)S(1)} all-gather(bf16[1,8,2048]{2,1,0:T(8,128)(2,1)S(1)} %slice-done), channel_id=2, replica_groups=mesh['groups'=2,'ctx'=16] {'ctx'}, dimensions={1}, use_global_device_ids=true | all-gather | bytes 557056 | tf_op jit(solution)/shard_map/all_gather | solution.py:100
  376.9 30.9 %collective-permute-done.6 = bf16[2,256,2048]{2,1,0:T(8,128)(2,1)} collective-permute-done((bf16[2,256,2048]{2,1,0:T(8,128)(2,1)}, bf16[2,256,2048]{2,1,0:T(8,128)(2,1)}, u32[]{:S(2)}, u32[]{:S(2)}) %collective-permute-start.6) | collective-permute-done | bytes 2097184 | tf_op jit(solution)/shard_map/ppermute | solution.py:16
  412.3 6.5 copy-done
  418.7 278.3 %while.8 = (s32[]{:T(128)}, bf16[16,256,128]{2,1,0:T(8,128)(2,1)}, s32[16]{0:T(128)S(1)}, s32[16]{0:T(128)S(1)}, bf16[3,256,2048]{2,1,0:T(8,128)(2,1)S(1)}, /*in...) while((s32[]{:T(128)}, bf16[16,256,128]{2,1,0:T(8,128)(2,1)}, ...), condition=%wide.region_3.4_spmd.clone.clone, body=%wide.region_0.3_spmd.clone.clone.sunk | while | flops 316772352 | bytes 48255728 | solution.py:90
  422.0 8.1 fusion.75
  439.4 8.1 fusion.75
  456.8 8.1 fusion.75
  474.2 8.1 fusion.75
  491.6 8.1 fusion.75
  509.0 8.1 fusion.75
  526.4 8.1 fusion.75
  543.8 8.1 fusion.75
  561.2 8.1 fusion.75
  578.6 8.1 fusion.75
  595.9 8.1 fusion.75
  613.3 8.1 fusion.75
  630.8 8.1 fusion.75
  648.1 8.1 fusion.75
  665.5 8.1 fusion.75
  682.9 8.1 fusion.75
  702.3 116.6 %all-to-all-start.2 = ((bf16[16,8,16]{2,1,0:T(8,128)(2,1)}), bf16[16,8,16]{2,1,0:T(8,128)(2,1)S(1)}, u32[]{:S(2)}, u32[]{:S(2)}) async-start(bf16[16,8,16]{2,1,0:T(8,128)(2,1)} %bitcast.20), calls=%async_computation.2 | async-start | bytes 65536 | tf_op jit(solution)/shard_map/all_to_all | solution.py:147
  842.2 11.3 %all-to-all-done = bf16[16,8,2048]{2,1,0:T(8,128)(2,1)S(1)} async-done(((bf16[16,8,2048]{2,1,0:T(8,128)(2,1)}), bf16[16,8,2048]{2,1,0:T(8,128)(2,1)S(1)}, u32[]{:S(2)}, u32[]{:S(2)}) %all-to-all-start) | async-done | bytes 524320 | tf_op jit(solution)/shard_map/all_to_all | solution.py:141
  (187 shorter events, 182.5 us)
Async XLA Ops:
  0.6 23.0 %copy-start.2 = (bf16[3,8,2048]{2,1,0:T(8,128)(2,1)S(1)}, bf16[3,8,2048]{2,1,0:T(8,128)(2,1)}, u32[]{:S(2)}) copy-start(bf16[3,8,2048]{2,1,0:T(8,128)(2,1)} %param.10) | copy-start | bytes 294916
  0.6 58.4 %slice-start = ((bf16[3,8,2048]{2,1,0:T(8,128)(2,1)}), bf16[1,8,2048]{2,1,0:T(8,128)(2,1)S(1)}, s32[]{:S(2)}) async-start(bf16[3,8,2048]{2,1,0:T(8,128)(2,1)} %param.10), calls=%async_computation.3 | async-start | bytes 65536 | tf_op jit(solution)/shard_map/slice | solution.py:100
  0.7 58.2 %copy-start.3 = (s32[16]{0:T(128)S(1)}, s32[16]{0:T(128)}, u32[]{:S(2)}) copy-start(s32[16]{0:T(128)} %param.11) | copy-start | bytes 196
  3.9 52.3 %collective-permute-start = (bf16[2,256,2048]{2,1,0:T(8,128)(2,1)}, bf16[2,256,2048]{2,1,0:T(8,128)(2,1)}, u32[]{:S(2)}, u32[]{:S(2)}) collective-permute-start(bf16[2,256,2048]{2,1,0:T(8,128)(2,1)} %slice.25), channel_id=1, source_target_pairs={{0,8},{1,9},{2,10},{3,11},{4,12},{5,13},{6,14},{7,15},{16,24},{17,... | collective-permute-start | bytes 6291464 | tf_op jit(solution)/shard_map/ppermute | solution.py:16
  11.2 348.9 %collective-permute-start.1 = (bf16[2,256,2048]{2,1,0:T(8,128)(2,1)}, bf16[2,256,2048]{2,1,0:T(8,128)(2,1)}, u32[]{:S(2)}, u32[]{:S(2)}) collective-permute-start(bf16[2,256,2048]{2,1,0:T(8,128)(2,1)} %slice.25), channel_id=1, source_target_pairs={{0,7},{1,8},{2,9},{3,10},{4,11},{5,12},{6,13},{7,14},{8,15},{16,23... | collective-permute-start | bytes 6291464 | tf_op jit(solution)/shard_map/ppermute | solution.py:16
  16.1 347.7 %collective-permute-start.2 = (bf16[2,256,2048]{2,1,0:T(8,128)(2,1)}, bf16[2,256,2048]{2,1,0:T(8,128)(2,1)}, u32[]{:S(2)}, u32[]{:S(2)}) collective-permute-start(bf16[2,256,2048]{2,1,0:T(8,128)(2,1)} %slice.25), channel_id=1, source_target_pairs={{0,6},{1,7},{2,8},{3,9},{4,10},{5,11},{6,12},{7,13},{8,14},{9,15},... | collective-permute-start | bytes 6291464 | tf_op jit(solution)/shard_map/ppermute | solution.py:16
  19.6 353.7 %collective-permute-start.3 = (bf16[2,256,2048]{2,1,0:T(8,128)(2,1)}, bf16[2,256,2048]{2,1,0:T(8,128)(2,1)}, u32[]{:S(2)}, u32[]{:S(2)}) collective-permute-start(bf16[2,256,2048]{2,1,0:T(8,128)(2,1)} %slice.25), channel_id=1, source_target_pairs={{0,5},{1,6},{2,7},{3,8},{4,9},{5,10},{6,11},{7,12},{8,13},{9,14},{... | collective-permute-start | bytes 6291464 | tf_op jit(solution)/shard_map/ppermute | solution.py:16
  22.2 352.8 %collective-permute-start.4 = (bf16[2,256,2048]{2,1,0:T(8,128)(2,1)}, bf16[2,256,2048]{2,1,0:T(8,128)(2,1)S(1)}, u32[]{:S(2)}, u32[]{:S(2)}) collective-permute-start(bf16[2,256,2048]{2,1,0:T(8,128)(2,1)} %slice.25), channel_id=1, source_target_pairs={{0,4},{1,5},{2,6},{3,7},{4,8},{5,9},{6,10},{7,11},{8,12},{9,13},{1... | collective-permute-start | bytes 6291464 | tf_op jit(solution)/shard_map/ppermute | solution.py:16
  56.2 319.0 %collective-permute-start.5 = (bf16[2,256,2048]{2,1,0:T(8,128)(2,1)}, bf16[2,256,2048]{2,1,0:T(8,128)(2,1)}, u32[]{:S(2)}, u32[]{:S(2)}) collective-permute-start(bf16[2,256,2048]{2,1,0:T(8,128)(2,1)} %slice.25), channel_id=1, source_target_pairs={{0,3},{1,4},{2,5},{3,6},{4,7},{5,8},{6,9},{7,10},{8,11},{9,12},{10... | collective-permute-start | bytes 6291464 | tf_op jit(solution)/shard_map/ppermute | solution.py:16
  360.0 47.8 %collective-permute-start.6 = (bf16[2,256,2048]{2,1,0:T(8,128)(2,1)}, bf16[2,256,2048]{2,1,0:T(8,128)(2,1)}, u32[]{:S(2)}, u32[]{:S(2)}) collective-permute-start(bf16[2,256,2048]{2,1,0:T(8,128)(2,1)} %slice.25), channel_id=1, source_target_pairs={{0,2},{1,3},{2,4},{3,5},{4,6},{5,7},{6,8},{7,9},{8,10},{9,11},{10,... | collective-permute-start | bytes 6291464 | tf_op jit(solution)/shard_map/ppermute | solution.py:16
  363.8 45.8 %collective-permute-start.7 = (bf16[2,256,2048]{2,1,0:T(8,128)(2,1)}, bf16[2,256,2048]{2,1,0:T(8,128)(2,1)}, u32[]{:S(2)}, u32[]{:S(2)}) collective-permute-start(bf16[2,256,2048]{2,1,0:T(8,128)(2,1)} %slice.25), channel_id=1, source_target_pairs={{0,1},{1,2},{2,3},{3,4},{4,5},{5,6},{6,7},{7,8},{8,9},{9,10},{10,1... | collective-permute-start | bytes 6291464 | tf_op jit(solution)/shard_map/ppermute | solution.py:16
  409.6 2.5 copy-start.1
  412.1 6.6 copy-start.5
  412.3 6.5 copy-start
  418.7 280.1 %copy-start.4 = (f32[2048]{0:T(1024)S(1)}, f32[2048]{0:T(1024)}, u32[]{:S(2)}) copy-start(f32[2048]{0:T(1024)} %param.9) | copy-start | bytes 24580
  702.3 123.3 %all-to-all-start.2 = ((bf16[16,8,16]{2,1,0:T(8,128)(2,1)}), bf16[16,8,16]{2,1,0:T(8,128)(2,1)S(1)}, u32[]{:S(2)}, u32[]{:S(2)}) async-start(bf16[16,8,16]{2,1,0:T(8,128)(2,1)} %bitcast.20), calls=%async_computation.2 | async-start | bytes 65536 | tf_op jit(solution)/shard_map/all_to_all | solution.py:147
  825.6 10.1 %all-to-all-start.1 = ((bf16[16,8,16]{2,1,0:T(8,128)(2,1)}), bf16[16,8,16]{2,1,0:T(8,128)(2,1)S(1)}, u32[]{:S(2)}, u32[]{:S(2)}) async-start(bf16[16,8,16]{2,1,0:T(8,128)(2,1)} %bitcast.6), calls=%async_computation.1 | async-start | bytes 65536 | tf_op jit(solution)/shard_map/all_to_all | solution.py:144
  835.7 17.8 %all-to-all-start = ((bf16[16,8,2048]{2,1,0:T(8,128)(2,1)}), bf16[16,8,2048]{2,1,0:T(8,128)(2,1)S(1)}, u32[]{:S(2)}, u32[]{:S(2)}) async-start(bf16[16,8,2048]{2,1,0:T(8,128)(2,1)} %convert_element_type.69), calls=%async_computation | async-start | bytes 1048576 | tf_op jit(solution)/shard_map/all_to_all | solution.py:141
where the time goes:
time: 856 us; the launch traced here: 855 us
  blocking collectives  301 us (35%)
  local copies, waits for them, and re-layouts  179 us (21%)
  starting transfers between devices  153 us (18%)
  waiting for transfers between devices  83.7 us (10%)
  matrix products  71.8 us (8%)
  loops' own time  35.4 us (4%)
  other arithmetic  30.3 us (4%)
    all_gather x1, blocking collectives, per_device(): gathered = lax.all_gather(cont_qkv[0], 'ctx', axis=0, tiled=True)  301 us
    slice x16, local copies, waits for them, and re-layouts, one_head(): values = lax.dynamic_slice_in_dim(band[1], offset, head_dim, 1)  130 us
    all_to_all x1, starting transfers between devices, per_device(): lax.all_to_all(totals.astype(jnp.bfloat16), 'ctx', split_axis=0, concat_a...  117 us
    ppermute x8, waiting for transfers between devices, shifted(): lax.ppermute(value, axis, [(source, source + steps) for source in range(i...  63.4 us
    dot_general x16, matrix products, one_head(): jnp.dot(weights, values, preferred_element_type=jnp.float32)  39.7 us
    another operation x1, loops' own time, per_device(): attended = lax.map(one_head, jnp.arange(head_count, dtype=jnp.int32))  35.4 us
    ppermute x8, starting transfers between devices, shifted(): lax.ppermute(value, axis, [(source, source + steps) for source in range(i...  29.1 us
    reduce_sum x16, other arithmetic, one_head(): jnp.sum(expo, axis=-1, keepdims=True)  27.1 us
  transfers between devices with their start and end apart: 11, of which 5 were waited for; matrix products, arithmetic and copies ran while one was open for 2% of the time, Pallas kernels for 0%

commit v1 on v0

--- a/solution.py
+++ b/solution.py
@@ -1,3 +1,4 @@
+import functools
 import math
 import jax
 import jax.numpy as jnp
@@ -8,6 +9,28 @@
 CLEN = 8
 EPSILON = 1e-06
 NEGATIVE = -1e30
+
+
+def put_the_terms(patch, d0):
+    spare = list(patch.shape[1:])
+    spare[d0] *= patch.shape[0]
+    inter = jnp.moveaxis(patch, 0, d0).reshape(spare)
+    return inter
+
+
+def apply_sheets(v0, lane_axis, dim_i):
+    total_devices = jax.lax.axis_size(lane_axis)
+    pile = [(c, (c + 1) % total_devices) for c in range(total_devices)]
+    panels = [v0]
+    while len(panels) < total_devices:
+        panels.append(jax.lax.ppermute(panels[-1], lane_axis, pile))
+    heard = jax.lax.axis_index(lane_axis)
+    panels = jnp.stack(panels, axis=0)[(heard - jnp.arange(total_devices)) % total_devices]
+    row_out = put_the_terms(panels, dim_i)
+    return row_out
+
+
+reach_set = functools.partial(apply_sheets, lane_axis="ctx", dim_i=0)
 
 
 def shifted(value, axis, steps):
@@ -97,7 +120,7 @@
         .reshape(length, head_count, head_dim)
     )
     cache_values = self_out.reshape(length, head_count, head_dim)
-    gathered = lax.all_gather(cont_qkv[0], "ctx", axis=0, tiled=True)
+    gathered = reach_set(cont_qkv[0])
     rows_all = gathered.shape[0]
     rows_here = cont_qkv.shape[1]
     conts_all = starts.shape[0]

time: 856 us -> 913 us (1.067)
  blocking collectives: 301 us -> 0 us
  starting transfers between devices: 153 us -> 395 us
  waiting for transfers between devices: 83.7 us -> 186 us
    all_gather x1 -> x0, blocking collectives: 301 us -> none  [per_device(): gathered = lax.all_gather(cont_qkv[0], 'ctx', axis=0, tiled=True)]
    ppermute x0 -> x15, starting transfers between devices: none -> 284 us  [apply_sheets(): panels.append(jax.lax.ppermute(panels[-1], lane_axis, pile))]
    ppermute x0 -> x15, waiting for transfers between devices: none -> 96 us  [apply_sheets(): panels.append(jax.lax.ppermute(panels[-1], lane_axis, pile))]
    all_to_all x1, starting transfers between devices: 117 us -> 65.7 us  [per_device(): lax.all_to_all(totals.astype(jnp.bfloat16), 'ctx', split_axis=0, concat_a...]
    unnamed x20 -> x35, local copies, waits for them, and re-layouts: 19.5 us -> 20.4 us
  transfers between devices with their start and end apart: 11 -> 26, of which waited for: 5 -> 21; matrix products, arithmetic and copies ran while one was open for 2% -> 2% of each run, Pallas kernels for 0% -> 0%
where the time goes in v1:
time: 913 us; the launch traced here: 911 us
  starting transfers between devices  395 us (43%)
  waiting for transfers between devices  186 us (20%)
  local copies, waits for them, and re-layouts  181 us (20%)
  matrix products  75 us (8%)
  loops' own time  40.9 us (4%)
  other arithmetic  32 us (4%)
    ppermute x15, starting transfers between devices, apply_sheets(): panels.append(jax.lax.ppermute(panels[-1], lane_axis, pile))  284 us
    slice x16, local copies, waits for them, and re-layouts, one_head(): values = lax.dynamic_slice_in_dim(band[1], offset, head_dim, 1)  130 us
    ppermute x15, waiting for transfers between devices, apply_sheets(): panels.append(jax.lax.ppermute(panels[-1], lane_axis, pile))  96 us
    ppermute x8, waiting for transfers between devices, shifted(): lax.ppermute(value, axis, [(source, source + steps) for source in range(i...  69.6 us
    all_to_all x1, starting transfers between devices, per_device(): lax.all_to_all(totals.astype(jnp.bfloat16), 'ctx', split_axis=0, concat_a...  65.7 us
    dot_general x16, matrix products, one_head(): jnp.dot(weights, values, preferred_element_type=jnp.float32)  41.1 us
    another operation x1, loops' own time, per_device(): attended = lax.map(one_head, jnp.arange(head_count, dtype=jnp.int32))  40.9 us
    ppermute x8, starting transfers between devices, shifted(): lax.ppermute(value, axis, [(source, source + steps) for source in range(i...  37.9 us
  transfers between devices with their start and end apart: 26, of which 21 were waited for; matrix products, arithmetic and copies ran while one was open for 2% of the time, Pallas kernels for 0%

profile of v1, /device:TPU:0, one launch (start us, length us, event | category | flops | bytes accessed | tf_op | source)
XLA Modules:
  0.0 910.6 jit_solution(17302333162454964007)
XLA Ops:
  33.1 31.3 %collective-permute-done.10 = bf16[8,2048]{1,0:T(8,128)(2,1)S(1)} collective-permute-done((bf16[8,2048]{1,0:T(8,128)(2,1)S(1)}, bf16[8,2048]{1,0:T(8,128)(2,1)S(1)}, u32[]{:S(2)}, u32[]{:S(2)}) %collective-permute-start.10) | collective-permute-done | bytes 32800 | tf_op jit(solution)/shard_map/ppermute | solution.py:26
  64.4 128.5 %collective-permute-start.11 = (bf16[8,2048]{1,0:T(8,128)(2,1)S(1)}, bf16[8,2048]{1,0:T(8,128)(2,1)S(1)}, u32[]{:S(2)}, u32[]{:S(2)}) collective-permute-start(bf16[8,2048]{1,0:T(8,128)(2,1)S(1)} %collective-permute-done.10), channel_id=1, source_target_pairs={{0,1},{1,2},{2,3},{3,4},{4,5},{5,6},{6,7},{7,8},{8,9},{9,10},{10,1... | collective-permute-start | bytes 98312 | tf_op jit(solution)/shard_map/ppermute | solution.py:26
  211.9 146.0 %collective-permute-start.15 = (bf16[8,2048]{1,0:T(8,128)(2,1)S(1)}, bf16[8,2048]{1,0:T(8,128)(2,1)S(1)}, u32[]{:S(2)}, u32[]{:S(2)}) collective-permute-start(bf16[8,2048]{1,0:T(8,128)(2,1)S(1)} %collective-permute-done.14), channel_id=1, source_target_pairs={{0,1},{1,2},{2,3},{3,4},{4,5},{5,6},{6,7},{7,8},{8,9},{9,10},{10,1... | collective-permute-start | bytes 98312 | tf_op jit(solution)/shard_map/ppermute | solution.py:26
  404.6 11.2 %collective-permute-start.5 = (bf16[2,256,2048]{2,1,0:T(8,128)(2,1)}, bf16[2,256,2048]{2,1,0:T(8,128)(2,1)}, u32[]{:S(2)}, u32[]{:S(2)}) collective-permute-start(bf16[2,256,2048]{2,1,0:T(8,128)(2,1)} %slice.25), channel_id=1, source_target_pairs={{0,3},{1,4},{2,5},{3,6},{4,7},{5,8},{6,9},{7,10},{8,11},{9,12},{10... | collective-permute-start | bytes 6291464 | tf_op jit(solution)/shard_map/ppermute | solution.py:39
  429.6 18.8 %collective-permute-done.4 = bf16[2,256,2048]{2,1,0:T(8,128)(2,1)} collective-permute-done((bf16[2,256,2048]{2,1,0:T(8,128)(2,1)}, bf16[2,256,2048]{2,1,0:T(8,128)(2,1)}, u32[]{:S(2)}, u32[]{:S(2)}) %collective-permute-start.4) | collective-permute-done | bytes 2097184 | tf_op jit(solution)/shard_map/ppermute | solution.py:39
  459.4 43.2 %collective-permute-done.6 = bf16[2,256,2048]{2,1,0:T(8,128)(2,1)} collective-permute-done((bf16[2,256,2048]{2,1,0:T(8,128)(2,1)}, bf16[2,256,2048]{2,1,0:T(8,128)(2,1)}, u32[]{:S(2)}, u32[]{:S(2)}) %collective-permute-start.6) | collective-permute-done | bytes 2097184 | tf_op jit(solution)/shard_map/ppermute | solution.py:39
  513.5 289.6 %while.8 = (s32[]{:T(128)}, bf16[16,256,128]{2,1,0:T(8,128)(2,1)}, s32[16]{0:T(128)S(1)}, s32[16]{0:T(128)S(1)}, bf16[3,256,2048]{2,1,0:T(8,128)(2,1)S(1)}, /*in...) while((s32[]{:T(128)}, bf16[16,256,128]{2,1,0:T(8,128)(2,1)}, ...), condition=%wide.region_3.4_spmd.clone.clone, body=%wide.region_0.3_spmd.clone.clone.sunk | while | flops 316772352 | bytes 48255728 | solution.py:113
  517.2 8.1 fusion.77
  535.3 8.1 fusion.77
  553.4 8.1 fusion.77
  571.6 8.1 fusion.77
  589.7 8.1 fusion.77
  607.8 8.1 fusion.77
  625.9 8.1 fusion.77
  644.0 8.1 fusion.77
  662.1 8.1 fusion.77
  680.2 8.1 fusion.77
  698.3 8.1 fusion.77
  716.4 8.1 fusion.77
  734.5 8.1 fusion.77
  770.7 8.1 fusion.77
  788.8 8.1 fusion.77
  809.2 65.7 %all-to-all-start.2 = ((bf16[16,8,16]{2,1,0:T(8,128)(2,1)}), bf16[16,8,16]{2,1,0:T(8,128)(2,1)S(1)}, u32[]{:S(2)}, u32[]{:S(2)}) async-start(bf16[16,8,16]{2,1,0:T(8,128)(2,1)} %bitcast.35), calls=%async_computation.2 | async-start | bytes 65536 | tf_op jit(solution)/shard_map/all_to_all | solution.py:170
  898.2 11.3 %all-to-all-done = bf16[16,8,2048]{2,1,0:T(8,128)(2,1)S(1)} async-done(((bf16[16,8,2048]{2,1,0:T(8,128)(2,1)}), bf16[16,8,2048]{2,1,0:T(8,128)(2,1)S(1)}, u32[]{:S(2)}, u32[]{:S(2)}) %all-to-all-start) | async-done | bytes 524320 | tf_op jit(solution)/shard_map/all_to_all | solution.py:164
  (233 shorter events, 291.0 us)
Async XLA Ops:
  3.9 400.7 %collective-permute-start = (bf16[2,256,2048]{2,1,0:T(8,128)(2,1)}, bf16[2,256,2048]{2,1,0:T(8,128)(2,1)S(1)}, u32[]{:S(2)}, u32[]{:S(2)}) collective-permute-start(bf16[2,256,2048]{2,1,0:T(8,128)(2,1)} %slice.25), channel_id=1, source_target_pairs={{0,8},{1,9},{2,10},{3,11},{4,12},{5,13},{6,14},{7,15},{16,24},{17,... | collective-permute-start | bytes 6291464 | tf_op jit(solution)/shard_map/ppermute | solution.py:39
  10.0 405.8 %collective-permute-start.1 = (bf16[2,256,2048]{2,1,0:T(8,128)(2,1)}, bf16[2,256,2048]{2,1,0:T(8,128)(2,1)}, u32[]{:S(2)}, u32[]{:S(2)}) collective-permute-start(bf16[2,256,2048]{2,1,0:T(8,128)(2,1)} %slice.25), channel_id=1, source_target_pairs={{0,7},{1,8},{2,9},{3,10},{4,11},{5,12},{6,13},{7,14},{8,15},{16,23... | collective-permute-start | bytes 6291464 | tf_op jit(solution)/shard_map/ppermute | solution.py:39
  14.8 403.5 %collective-permute-start.2 = (bf16[2,256,2048]{2,1,0:T(8,128)(2,1)}, bf16[2,256,2048]{2,1,0:T(8,128)(2,1)}, u32[]{:S(2)}, u32[]{:S(2)}) collective-permute-start(bf16[2,256,2048]{2,1,0:T(8,128)(2,1)} %slice.25), channel_id=1, source_target_pairs={{0,6},{1,7},{2,8},{3,9},{4,10},{5,11},{6,12},{7,13},{8,14},{9,15},... | collective-permute-start | bytes 6291464 | tf_op jit(solution)/shard_map/ppermute | solution.py:39
  18.3 409.5 %collective-permute-start.3 = (bf16[2,256,2048]{2,1,0:T(8,128)(2,1)}, bf16[2,256,2048]{2,1,0:T(8,128)(2,1)}, u32[]{:S(2)}, u32[]{:S(2)}) collective-permute-start(bf16[2,256,2048]{2,1,0:T(8,128)(2,1)} %slice.25), channel_id=1, source_target_pairs={{0,5},{1,6},{2,7},{3,8},{4,9},{5,10},{6,11},{7,12},{8,13},{9,14},{... | collective-permute-start | bytes 6291464 | tf_op jit(solution)/shard_map/ppermute | solution.py:39
  20.9 6.1 collective-permute-start.8
  27.0 6.0 collective-permute-start.9
  33.1 31.3 %collective-permute-start.10 = (bf16[8,2048]{1,0:T(8,128)(2,1)S(1)}, bf16[8,2048]{1,0:T(8,128)(2,1)S(1)}, u32[]{:S(2)}, u32[]{:S(2)}) collective-permute-start(bf16[8,2048]{1,0:T(8,128)(2,1)S(1)} %collective-permute-done.9), channel_id=1, source_target_pairs={{0,1},{1,2},{2,3},{3,4},{4,5},{5,6},{6,7},{7,8},{8,9},{9,10},{10,1... | collective-permute-start | bytes 98312 | tf_op jit(solution)/shard_map/ppermute | solution.py:26
  64.4 129.4 %collective-permute-start.11 = (bf16[8,2048]{1,0:T(8,128)(2,1)S(1)}, bf16[8,2048]{1,0:T(8,128)(2,1)S(1)}, u32[]{:S(2)}, u32[]{:S(2)}) collective-permute-start(bf16[8,2048]{1,0:T(8,128)(2,1)S(1)} %collective-permute-done.10), channel_id=1, source_target_pairs={{0,1},{1,2},{2,3},{3,4},{4,5},{5,6},{6,7},{7,8},{8,9},{9,10},{10,1... | collective-permute-start | bytes 98312 | tf_op jit(solution)/shard_map/ppermute | solution.py:26
  193.8 6.0 collective-permute-start.12
  199.8 6.0 collective-permute-start.13
  205.9 6.0 collective-permute-start.14
  211.9 146.9 %collective-permute-start.15 = (bf16[8,2048]{1,0:T(8,128)(2,1)S(1)}, bf16[8,2048]{1,0:T(8,128)(2,1)S(1)}, u32[]{:S(2)}, u32[]{:S(2)}) collective-permute-start(bf16[8,2048]{1,0:T(8,128)(2,1)S(1)} %collective-permute-done.14), channel_id=1, source_target_pairs={{0,1},{1,2},{2,3},{3,4},{4,5},{5,6},{6,7},{7,8},{8,9},{9,10},{10,1... | collective-permute-start | bytes 98312 | tf_op jit(solution)/shard_map/ppermute | solution.py:26
  358.8 7.0 collective-permute-start.16
  365.7 6.0 collective-permute-start.17
  371.8 6.0 collective-permute-start.18
  377.8 6.0 collective-permute-start.19
  383.8 6.0 collective-permute-start.20
  401.9 46.4 %collective-permute-start.4 = (bf16[2,256,2048]{2,1,0:T(8,128)(2,1)}, bf16[2,256,2048]{2,1,0:T(8,128)(2,1)}, u32[]{:S(2)}, u32[]{:S(2)}) collective-permute-start(bf16[2,256,2048]{2,1,0:T(8,128)(2,1)} %slice.25), channel_id=1, source_target_pairs={{0,4},{1,5},{2,6},{3,7},{4,8},{5,9},{6,10},{7,11},{8,12},{9,13},{1... | collective-permute-start | bytes 6291464 | tf_op jit(solution)/shard_map/ppermute | solution.py:39
  404.6 53.1 %collective-permute-start.5 = (bf16[2,256,2048]{2,1,0:T(8,128)(2,1)}, bf16[2,256,2048]{2,1,0:T(8,128)(2,1)}, u32[]{:S(2)}, u32[]{:S(2)}) collective-permute-start(bf16[2,256,2048]{2,1,0:T(8,128)(2,1)} %slice.25), channel_id=1, source_target_pairs={{0,3},{1,4},{2,5},{3,6},{4,7},{5,8},{6,9},{7,10},{8,11},{9,12},{10... | collective-permute-start | bytes 6291464 | tf_op jit(solution)/shard_map/ppermute | solution.py:39
  415.8 86.9 %collective-permute-start.6 = (bf16[2,256,2048]{2,1,0:T(8,128)(2,1)}, bf16[2,256,2048]{2,1,0:T(8,128)(2,1)}, u32[]{:S(2)}, u32[]{:S(2)}) collective-permute-start(bf16[2,256,2048]{2,1,0:T(8,128)(2,1)} %slice.25), channel_id=1, source_target_pairs={{0,2},{1,3},{2,4},{3,5},{4,6},{5,7},{6,8},{7,9},{8,10},{9,11},{10,... | collective-permute-start | bytes 6291464 | tf_op jit(solution)/shard_map/ppermute | solution.py:39
  418.4 86.0 %collective-permute-start.7 = (bf16[2,256,2048]{2,1,0:T(8,128)(2,1)}, bf16[2,256,2048]{2,1,0:T(8,128)(2,1)}, u32[]{:S(2)}, u32[]{:S(2)}) collective-permute-start(bf16[2,256,2048]{2,1,0:T(8,128)(2,1)} %slice.25), channel_id=1, source_target_pairs={{0,1},{1,2},{2,3},{3,4},{4,5},{5,6},{6,7},{7,8},{8,9},{9,10},{10,1... | collective-permute-start | bytes 6291464 | tf_op jit(solution)/shard_map/ppermute | solution.py:39
  809.2 72.4 %all-to-all-start.2 = ((bf16[16,8,16]{2,1,0:T(8,128)(2,1)}), bf16[16,8,16]{2,1,0:T(8,128)(2,1)S(1)}, u32[]{:S(2)}, u32[]{:S(2)}) async-start(bf16[16,8,16]{2,1,0:T(8,128)(2,1)} %bitcast.35), calls=%async_computation.2 | async-start | bytes 65536 | tf_op jit(solution)/shard_map/all_to_all | solution.py:170
  881.6 10.1 %all-to-all-start.1 = ((bf16[16,8,16]{2,1,0:T(8,128)(2,1)}), bf16[16,8,16]{2,1,0:T(8,128)(2,1)S(1)}, u32[]{:S(2)}, u32[]{:S(2)}) async-start(bf16[16,8,16]{2,1,0:T(8,128)(2,1)} %bitcast.21), calls=%async_computation.1 | async-start | bytes 65536 | tf_op jit(solution)/shard_map/all_to_all | solution.py:167
  891.7 17.8 %all-to-all-start = ((bf16[16,8,2048]{2,1,0:T(8,128)(2,1)}), bf16[16,8,2048]{2,1,0:T(8,128)(2,1)S(1)}, u32[]{:S(2)}, u32[]{:S(2)}) async-start(bf16[16,8,2048]{2,1,0:T(8,128)(2,1)} %convert_element_type.69), calls=%async_computation | async-start | bytes 1048576 | tf_op jit(solution)/shard_map/all_to_all | solution.py:164
  (8 other events, 360.0 us)
